TPU v7x, 512 devices: a whole 4x8x8 slice. The times are simulated.
512 devices in a mesh: space: 128 (over y_hi, x, z, core), filt: 4 (over y_lo).
Axes of the slice: x: 4, y: 8 (y_hi: 2, y_lo: 4; y = y_hi * 4 + y_lo), z: 8, core: 2. Of those that a mesh axis runs over, the one named last changes fastest.
Arguments:
- image: bfloat16 [96, 512, 1024], P(None, 'space', 'filt'), may hold values from -6 to 6
- cotangent: bfloat16 [96, 512, 1024], P(None, 'space', 'filt'), may hold values from -6 to 6
- kernel: float32 [96, 7, 7], replicated, may hold values from -0.875 to 0.875
- dw_bias: float32 [96], replicated, may hold values from -0.5 to 0.5
- layer_norm_gain: float32 [96], replicated, may hold values from 0.5 to 1.5
- layer_norm_bias: float32 [96], replicated, may hold values from -3 to 3
- w_expand: bfloat16 [384, 96], replicated, may hold values from -0.625 to 0.625
- b_expand: bfloat16 [384], replicated, may hold values from -3 to 3
- w_reduce: bfloat16 [384, 96], replicated, may hold values from -0.3125 to 0.3125
- b_reduce: float32 [96], replicated, may hold values from -3 to 3
- layer_scale: float32 [96], replicated, may hold values from 0.2 to 1
Outputs:
- output: bfloat16 [96, 512, 1024], P(None, 'space', 'filt')
- image_grad: bfloat16 [96, 512, 1024], P(None, 'space', 'filt')
- kernel_grad: float32 [96, 7, 7], replicated
- dw_bias_grad: float32 [96], replicated
- gain_grad: float32 [96], replicated
- ln_bias_grad: float32 [96], replicated
- expand_grad: float32 [384, 96], P('filt')
- expand_bias_grad: float32 [384], P('filt')
- reduce_grad: float32 [384, 96], P('filt')
- reduce_bias_grad: float32 [96], replicated
- scale_grad: float32 [96], replicated
All inputs are finite; a program needn't handle non-finite values.
Results may differ from a plain program's by a relative error of at most 0.011.
Values may be sent and summed in bfloat16 or wider, within the bound.
A program may use at most 64 MiB of HBM per device.

v0:
```python
import math
import jax
import jax.numpy as jnp
from jax import lax
from jax.sharding import PartitionSpec as P


def padded_2(x, sides, width):
    for axis, dim in sides:
        size, length = (lax.axis_size(axis), x.shape[dim])
        up = [(i, (i + 1) % size) for i in range(size - 1)]
        down = [(j, i) for i, j in up]
        last = lax.slice_in_dim(x, length - width, length, axis=dim)
        initial = lax.slice_in_dim(x, 0, width, axis=dim)
        before = lax.ppermute(last, axis, up)
        after = lax.ppermute(initial, axis, down)
        x = jnp.concatenate([before, x, after], axis=dim)
    return x


def depthwise(padded, kernel, row_count, col_count):
    total = jnp.zeros((padded.shape[0], row_count, col_count), jnp.float32)
    for shift_row in range(7):
        for shift_col in range(7):
            piece = padded[
                :, shift_row : shift_row + row_count, shift_col : shift_col + col_count
            ].astype(jnp.float32)
            total = total + kernel[:, shift_row, shift_col][:, None, None] * piece
    return total


def conv_back(padded, kernel, row_count, col_count):
    total = jnp.zeros((padded.shape[0], row_count, col_count), jnp.float32)
    for shift_row in range(7):
        for shift_col in range(7):
            piece = padded[
                :,
                6 - shift_row : 6 - shift_row + row_count,
                6 - shift_col : 6 - shift_col + col_count,
            ].astype(jnp.float32)
            total = total + kernel[:, shift_row, shift_col][:, None, None] * piece
    return total


def kernel_terms(padded, convolution_gradient, row_count, col_count):
    lines = []
    for shift_row in range(7):
        entries = []
        for shift_col in range(7):
            piece = padded[
                :, shift_row : shift_row + row_count, shift_col : shift_col + col_count
            ].astype(jnp.float32)
            entries.append(jnp.sum(piece * convolution_gradient, axis=(1, 2)))
        lines.append(jnp.stack(entries, axis=1))
    return jnp.stack(lines, axis=1)


def gelu_exact(value):
    return value * (1.0 + jax.scipy.special.erf(value / math.sqrt(2.0))) * 0.5


def gelu_slope(value):
    return (1.0 + jax.scipy.special.erf(value / math.sqrt(2.0))) * 0.5 + value * jnp.exp(
        -0.5 * value * value
    ) / math.sqrt(2.0 * math.pi)


def shards(
    image,
    cotangent,
    kernel,
    dw_bias,
    layer_norm_gain,
    layer_norm_bias,
    w_expand,
    b_expand,
    w_reduce,
    b_reduce,
    layer_scale,
):
    channels, row_count, col_count = image.shape
    panel_rows = w_expand.shape[0] // lax.axis_size("filt")
    tok_count = row_count * col_count
    padded = padded_2(image, (("space", 1), ("filt", 2)), 3)
    conv = depthwise(padded, kernel, row_count, col_count)
    conv = conv + dw_bias[:, None, None]
    flat = conv.reshape(channels, tok_count)
    average = jnp.mean(flat, axis=0, keepdims=True)
    mean_removed = flat - average
    inverse_deviation = lax.rsqrt(
        jnp.mean(mean_removed * mean_removed, axis=0, keepdims=True) + 1e-06
    )
    standardized_input = mean_removed * inverse_deviation
    normalized_input = (
        standardized_input * layer_norm_gain[:, None] + layer_norm_bias[:, None]
    ).astype(jnp.bfloat16)
    hidden = (
        jnp.dot(w_expand, normalized_input, preferred_element_type=jnp.float32)
        + b_expand.astype(jnp.float32)[:, None]
    )
    active = gelu_exact(hidden).astype(jnp.bfloat16)
    branch = (
        lax.dot_general(
            w_reduce, active, (((0,), (0,)), ((), ())), preferred_element_type=jnp.float32
        )
        + b_reduce[:, None]
    )
    resid = image.reshape(channels, tok_count).astype(jnp.float32)
    output = (
        (resid + layer_scale[:, None] * branch)
        .astype(jnp.bfloat16)
        .reshape(channels, row_count, col_count)
    )
    cot_flat = cotangent.reshape(channels, tok_count).astype(jnp.float32)
    scaled = layer_scale[:, None] * cot_flat
    g_scale = jnp.sum(cot_flat * branch, axis=1)
    g_rbias = jnp.sum(scaled, axis=1)
    d_branch = scaled.astype(jnp.bfloat16)
    g_reduce = lax.dot_general(
        active, d_branch, (((1,), (1,)), ((), ())), preferred_element_type=jnp.float32
    )
    d_active = jnp.dot(w_reduce, d_branch, preferred_element_type=jnp.float32)
    d_hidden = (d_active * gelu_slope(hidden)).astype(jnp.bfloat16)
    g_ebias = jnp.sum(d_hidden.astype(jnp.float32), axis=1)
    g_expand = lax.dot_general(
        d_hidden, normalized_input, (((1,), (1,)), ((), ())), preferred_element_type=jnp.float32
    )
    normalized_gradient = lax.dot_general(
        w_expand, d_hidden, (((0,), (0,)), ((), ())), preferred_element_type=jnp.float32
    )
    norm_gain_gradient = jnp.sum(normalized_gradient * standardized_input, axis=1)
    g_lbias = jnp.sum(normalized_gradient, axis=1)
    standardized_gradient = normalized_gradient * layer_norm_gain[:, None]
    convolution_gradient = inverse_deviation * (
        standardized_gradient
        - jnp.mean(standardized_gradient, axis=0, keepdims=True)
        - standardized_input
        * jnp.mean(standardized_gradient * standardized_input, axis=0, keepdims=True)
    )
    convolution_gradient = convolution_gradient.astype(jnp.bfloat16).reshape(
        channels, row_count, col_count
    )
    d_float = convolution_gradient.astype(jnp.float32)
    g_dbias = jnp.sum(d_float, axis=(1, 2))
    padded_grad = padded_2(convolution_gradient, (("space", 1), ("filt", 2)), 3)
    back = conv_back(padded_grad, kernel, row_count, col_count)
    image_grad = (cotangent.astype(jnp.float32) + back).astype(jnp.bfloat16)
    g_kernel = kernel_terms(padded, d_float, row_count, col_count)
    factor = 1.0 / math.sqrt(tok_count * lax.axis_size("space") * lax.axis_size("filt"))
    (
        g_reduce,
        g_expand,
        g_ebias,
        g_kernel,
        g_dbias,
        norm_gain_gradient,
        g_lbias,
        g_scale,
        g_rbias,
    ) = lax.psum(
        (
            g_reduce,
            g_expand,
            g_ebias,
            g_kernel,
            g_dbias,
            norm_gain_gradient,
            g_lbias,
            g_scale,
            g_rbias,
        ),
        ("space", "filt"),
    )
    start = lax.axis_index("filt") * panel_rows
    g_reduce = lax.dynamic_slice_in_dim(g_reduce, start, panel_rows, 0)
    g_expand = lax.dynamic_slice_in_dim(g_expand, start, panel_rows, 0)
    g_ebias = lax.dynamic_slice_in_dim(g_ebias, start, panel_rows, 0)
    return (
        output,
        image_grad,
        g_kernel * factor,
        g_dbias * factor,
        norm_gain_gradient * factor,
        g_lbias * factor,
        g_expand * factor,
        g_ebias * factor,
        g_reduce * factor,
        g_rbias * factor,
        g_scale * factor,
    )


def solution(mesh):
    in_specs = (
        P(None, "space", "filt"),
        P(None, "space", "filt"),
        P(),
        P(),
        P(),
        P(),
        P(),
        P(),
        P(),
        P(),
        P(),
    )
    out_specs = (
        P(None, "space", "filt"),
        P(None, "space", "filt"),
        P(),
        P(),
        P(),
        P(),
        P("filt", None),
        P("filt"),
        P("filt", None),
        P(),
        P(),
    )
    return jax.shard_map(shards, mesh=mesh, in_specs=in_specs, out_specs=out_specs, check_vma=False)
```

profile of v0, /device:TPU:1, one launch (start us, length us, event | category | flops | bytes accessed | tf_op | source)
XLA Modules:
  0.0 504.9 jit_solution(11829889516771855415)
XLA Ops:
  8.5 5.5 %collective-permute-start = (bf16[96,3,256]{2,1,0:T(4,128)(2,1)S(1)}, bf16[96,3,256]{2,1,0:T(4,128)(2,1)S(1)}, u32[]{:S(2)}, u32[]{:S(2)}) collective-permute-start(bf16[96,3,256]{2,1,0:T(4,128)(2,1)S(1)} %get-tuple-element.98), channel_id=1, source_target_pairs={{0,4},{4,8},{8,12},{12,16},{16,20},{20,24},{24,28},{28,32},{32,36}... | collective-permute-start | bytes 442376 | tf_op jit(solution)/shard_map/ppermute | solution.py:15
  14.0 4.7 collective-permute-start.1
  19.7 1.6 slice_bitcast_fusion.47
  21.5 1.5 slice_bitcast_fusion.46
  23.0 1.6 pad_maximum_fusion.2
  27.4 2.0 multiply_reduce_fusion.1
  30.5 6.1 %collective-permute-done.2 = bf16[96,10,3]{2,1,0:T(8,128)(2,1)S(1)} collective-permute-done((bf16[96,10,3]{2,1,0:T(8,128)(2,1)S(1)}, bf16[96,10,3]{2,1,0:T(8,128)(2,1)S(1)}, u32[]{:S(2)}, u32[]{:S(2)}) %collective-permute-start.2) | collective-permute-done | bytes 5792 | tf_op jit(solution)/shard_map/ppermute | solution.py:15
  37.4 1.5 collective-permute-done.3
  38.9 3.4 maximum_maximum_fusion
  42.7 11.5 %fusion.134 = (f32[4,256]{1,0:T(4,128)S(1)}, f32[96,4,256]{2,1,0:T(4,128)S(1)}) fusion(f32[96]{0:T(128)S(1)} %copy-done.92, bf16[96,10,259]{2,1,0:T(8,128)(2,1)S(1)} %get-tuple-element.93, f32[96]{0:T(128)S(1)} %copy-done.82, f32[96]{0:T(128)S(1)} %copy-done.84, f32[96]{0:T(128)S(1)} %get-tuple-element.101, ...), kind=kLoop, calls=%fused_computation.346 | loop fusion | flops 16317440 | bytes 9165568 | tf_op jit(solution)/shard_map/reduce_sum | solution.py:88
  54.6 1.5 fusion.9
  56.1 1.5 convert_reduce_fusion
  62.3 7.8 %fusion.115 = (f32[96]{0:T(128)}, f32[96]{0:T(128)}, f32[96]{0:T(128)}, f32[96]{0:T(128)}, f32[96]{0:T(128)}, /*index=5*/f32[96]{0:T(128)}, f32[96]{0:T(128)}, f...) fusion(bf16[96,4,256]{2,1,0:T(4,128)(2,1)S(1)} %reshape.89, ...), kind=kLoop, calls=%fused_computation.241 | loop fusion | flops 5404992 | bytes 3742464 | tf_op jit(solution)/shard_map/reduce_sum | solution.py:53
  70.0 9.8 %fusion.119 = (f32[96]{0:T(128)}, f32[96]{0:T(128)}, f32[96]{0:T(128)}, f32[96]{0:T(128)}, f32[96]{0:T(128)}, /*index=5*/f32[96]{0:T(128)}, f32[96]{0:T(128)}, f...) fusion(bf16[96,4,256]{2,1,0:T(4,128)(2,1)S(1)} %reshape.89, ...), kind=kLoop, calls=%fused_computation.245 | loop fusion | flops 5404992 | bytes 3742464 | tf_op jit(solution)/shard_map/reduce_sum | solution.py:53
  79.8 2.8 fusion.73
  84.7 5.9 %fusion.118 = (f32[96]{0:T(128)}, f32[96]{0:T(128)}, f32[96]{0:T(128)}, f32[96]{0:T(128)}, f32[96]{0:T(128)}, /*index=5*/f32[96]{0:T(128)}, f32[96]{0:T(128)}, f32[96]{0:T(128)}, f32[96]{0:T(128)}, f32[96]{0:T(128)}) fusion(bf16[96,4,256]{2,1,0:T(4,128)(2,1)S(1)} %reshape.89, bf16[96,10,259]{2,1,0:T(8,128)(2,1)S(1)} %get-tuple-element.93, ...), kind=kLoop, calls=%fused_computation.244 | loop fusion | flops 4815936 | bytes 1281792 | tf_op jit(solution)/shard_map/reduce_sum | solution.py:53
  97.4 108.8 %all-reduce = (f32[96,7,7]{0,2,1:T(8,128)S(1)}, f32[96]{0:T(128)S(1)}, f32[96]{0:T(128)S(1)}, f32[96]{0:T(128)S(1)}, f32[384]{0:T(512)S(1)}, /*index=5*/f32[96]{0:T(128)S(1)}, f32[96]{0:T(128)S(1)}) all-reduce(f32[96,7,7]{0,2,1:T(8,128)S(1)} %constant_dynamic-update-slice_fusion, ...), channel_id=1, replica_groups=mesh['space'=128,'filt'=4] {'space','filt'}, use_global_device_ids=true, to_apply=%region_53.0 | all-reduce | flops 5568 | bytes 44544 | tf_op jit(solution)/shard_map/psum | solution.py:160
  208.9 2.5 collective-permute-start.4
  211.4 1.9 collective-permute-start.5
  215.3 3.1 collective-permute-done.5
  220.4 4.0 collective-permute-start.7
  224.4 257.4 %all-reduce.4.cloned.1.call-done = (f32[384,96]{1,0:T(8,128)}, f32[384,96]{1,0:T(8,128)}) async-done(((f32[384,96]{1,0:T(8,128)}, f32[384,96]{1,0:T(8,128)}), (f32[384,96]{1,0:T(8,128)}, f32[384,96]{1,0:T(8,128)})) %all-reduce.4.cloned.1.call-update) | async-done | bytes 294928 | tf_op jit(solution)/shard_map/psum | solution.py:160
  483.7 2.3 pad_maximum_fusion.1
  486.3 11.7 %add_convert_fusion = bf16[96,4,256]{2,1,0:T(4,128)(2,1)} fusion(bf16[96,4,256]{2,1,0:T(4,128)(2,1)S(1)} %reshape.89, bf16[96,3,256]{2,1,0:T(4,128)(2,1)S(1)} %collective-permute-done.4, bf16[96,3,256]{2,1,0:T(4,128)(2,1)S(1)} %collective-permute-done.5, bf16[96,10,259]{2,1,0:T(8,128)(2,1)S(1)} %get-tuple-element.91, ...), kind=kLoop, calls=%fused_computation.252 | loop fusion | flops 16416768 | bytes 9161088 | tf_op jit(solution)/shard_map/convert_element_type | solution.py:147
  (242 shorter events, 28.7 us)
Async XLA Ops:
  7.2 47.4 %copy-start = (bf16[384,96]{0,1:T(8,128)(2,1)S(1)}, bf16[384,96]{0,1:T(8,128)(2,1)}, u32[]{:S(2)}) copy-start(bf16[384,96]{0,1:T(8,128)(2,1)} %param.17) | copy-start | bytes 221188
  7.2 474.7 %all-reduce.4.cloned.1.call-start = ((), (), s32[]{:S(2)}) async-start(), calls=%async_computation | async-start | bytes 786432 | tf_op jit(solution)/shard_map/psum | solution.py:160
  8.5 14.5 %collective-permute-start = (bf16[96,3,256]{2,1,0:T(4,128)(2,1)S(1)}, bf16[96,3,256]{2,1,0:T(4,128)(2,1)S(1)}, u32[]{:S(2)}, u32[]{:S(2)}) collective-permute-start(bf16[96,3,256]{2,1,0:T(4,128)(2,1)S(1)} %get-tuple-element.98), channel_id=1, source_target_pairs={{0,4},{4,8},{8,12},{12,16},{16,20},{20,24},{24,28},{28,32},{32,36}... | collective-permute-start | bytes 442376 | tf_op jit(solution)/shard_map/ppermute | solution.py:15
  14.0 9.0 %collective-permute-start.1 = (bf16[96,3,256]{2,1,0:T(4,128)(2,1)S(1)}, bf16[96,3,256]{2,1,0:T(4,128)(2,1)S(1)}, u32[]{:S(2)}, u32[]{:S(2)}) collective-permute-start(bf16[96,3,256]{2,1,0:T(4,128)(2,1)S(1)} %get-tuple-element.99), channel_id=1, source_target_pairs={{4,0},{8,4},{12,8},{16,12},{20,16},{24,20},{28,24},{32,28},{36,32}... | collective-permute-start | bytes 442376 | tf_op jit(solution)/shard_map/ppermute | solution.py:16
  19.7 22.7 %copy-start.16 = (f32[96]{0:T(128)}, f32[96]{0:T(128)S(1)}, u32[]{:S(2)}) copy-start(f32[96]{0:T(128)S(1)} %get-tuple-element.114) | copy-start | bytes 1156
  19.7 22.7 %copy-start.18 = (f32[96]{0:T(128)}, f32[96]{0:T(128)S(1)}, u32[]{:S(2)}) copy-start(f32[96]{0:T(128)S(1)} %get-tuple-element.115) | copy-start | bytes 1156
  19.7 22.7 %copy-start.20 = (f32[96]{0:T(128)}, f32[96]{0:T(128)S(1)}, u32[]{:S(2)}) copy-start(f32[96]{0:T(128)S(1)} %get-tuple-element.116) | copy-start | bytes 1156
  19.7 22.7 %copy-start.22 = (f32[96]{0:T(128)}, f32[96]{0:T(128)S(1)}, u32[]{:S(2)}) copy-start(f32[96]{0:T(128)S(1)} %get-tuple-element.117) | copy-start | bytes 1156
  19.7 22.7 %copy-start.24 = (f32[96]{0:T(128)}, f32[96]{0:T(128)S(1)}, u32[]{:S(2)}) copy-start(f32[96]{0:T(128)S(1)} %get-tuple-element.118) | copy-start | bytes 1156
  21.3 21.1 %copy-start.28 = (f32[96]{0:T(128)}, f32[96]{0:T(128)S(1)}, u32[]{:S(2)}) copy-start(f32[96]{0:T(128)S(1)} %get-tuple-element.120) | copy-start | bytes 1156
  21.3 21.1 %copy-start.30 = (f32[96]{0:T(128)}, f32[96]{0:T(128)S(1)}, u32[]{:S(2)}) copy-start(f32[96]{0:T(128)S(1)} %get-tuple-element.121) | copy-start | bytes 1156
  21.4 21.1 %copy-start.32 = (f32[96]{0:T(128)}, f32[96]{0:T(128)S(1)}, u32[]{:S(2)}) copy-start(f32[96]{0:T(128)S(1)} %get-tuple-element.122) | copy-start | bytes 1156
  21.4 21.1 %copy-start.34 = (f32[96]{0:T(128)}, f32[96]{0:T(128)S(1)}, u32[]{:S(2)}) copy-start(f32[96]{0:T(128)S(1)} %get-tuple-element.123) | copy-start | bytes 1156
  21.4 21.1 %copy-start.36 = (f32[96]{0:T(128)}, f32[96]{0:T(128)S(1)}, u32[]{:S(2)}) copy-start(f32[96]{0:T(128)S(1)} %get-tuple-element.124) | copy-start | bytes 1156
  21.4 21.1 %copy-start.38 = (f32[96]{0:T(128)}, f32[96]{0:T(128)S(1)}, u32[]{:S(2)}) copy-start(f32[96]{0:T(128)S(1)} %get-tuple-element.125) | copy-start | bytes 1156
  24.8 11.9 %collective-permute-start.2 = (bf16[96,10,3]{2,1,0:T(8,128)(2,1)S(1)}, bf16[96,10,3]{2,1,0:T(8,128)(2,1)S(1)}, u32[]{:S(2)}, u32[]{:S(2)}) collective-permute-start(bf16[96,10,3]{2,1,0:T(8,128)(2,1)S(1)} %get-tuple-element.88), channel_id=1, source_target_pairs={{0,1},{1,2},{2,3},{4,5},{5,6},{6,7},{8,9},{9,10},{10,11},{12,13},{... | collective-permute-start | bytes 17288 | tf_op jit(solution)/shard_map/ppermute | solution.py:15
  26.1 12.8 %collective-permute-start.3 = (bf16[96,10,3]{2,1,0:T(8,128)(2,1)S(1)}, bf16[96,10,3]{2,1,0:T(8,128)(2,1)}, u32[]{:S(2)}, u32[]{:S(2)}) collective-permute-start(bf16[96,10,3]{2,1,0:T(8,128)(2,1)S(1)} %get-tuple-element.89), channel_id=1, source_target_pairs={{1,0},{2,1},{3,2},{5,4},{6,5},{7,6},{9,8},{10,9},{11,10},{13,12},{... | collective-permute-start | bytes 17288 | tf_op jit(solution)/shard_map/ppermute | solution.py:16
  29.5 26.6 %copy-start.4 = (f32[12,8,4,256]{3,1,2,0:T(8,128)}, f32[12,8,4,256]{3,1,2,0:T(8,128)S(1)}, u32[]{:S(2)}) copy-start(f32[12,8,4,256]{3,1,2,0:T(8,128)S(1)} %copy.26) | copy-start | bytes 1179652
  90.6 118.3 %copy-start.12 = (bf16[96,3,256]{2,1,0:T(4,128)(2,1)S(1)}, bf16[96,3,256]{2,1,0:T(4,128)(2,1)}, u32[]{:S(2)}) copy-start(bf16[96,3,256]{2,1,0:T(4,128)(2,1)} %get-tuple-element.97) | copy-start | bytes 442372
  90.6 120.8 %copy-start.11 = (bf16[96,3,256]{2,1,0:T(4,128)(2,1)S(1)}, bf16[96,3,256]{2,1,0:T(4,128)(2,1)}, u32[]{:S(2)}) copy-start(bf16[96,3,256]{2,1,0:T(4,128)(2,1)} %get-tuple-element.96) | copy-start | bytes 442372
  208.9 6.4 %collective-permute-start.4 = (bf16[96,3,256]{2,1,0:T(4,128)(2,1)S(1)}, bf16[96,3,256]{2,1,0:T(4,128)(2,1)S(1)}, u32[]{:S(2)}, u32[]{:S(2)}) collective-permute-start(bf16[96,3,256]{2,1,0:T(4,128)(2,1)S(1)} %copy-done.12), channel_id=1, source_target_pairs={{0,4},{4,8},{8,12},{12,16},{16,20},{20,24},{24,28},{28,32},{32,36}... | collective-permute-start | bytes 442376 | tf_op jit(solution)/shard_map/ppermute | solution.py:15
  211.4 7.0 %collective-permute-start.5 = (bf16[96,3,256]{2,1,0:T(4,128)(2,1)S(1)}, bf16[96,3,256]{2,1,0:T(4,128)(2,1)S(1)}, u32[]{:S(2)}, u32[]{:S(2)}) collective-permute-start(bf16[96,3,256]{2,1,0:T(4,128)(2,1)S(1)} %copy-done.11), channel_id=1, source_target_pairs={{4,0},{8,4},{12,8},{16,12},{20,16},{24,20},{28,24},{32,28},{36,32}... | collective-permute-start | bytes 442376 | tf_op jit(solution)/shard_map/ppermute | solution.py:16
  219.1 264.6 %collective-permute-start.6 = (bf16[96,10,3]{2,1,0:T(8,128)(2,1)S(1)}, bf16[96,10,3]{2,1,0:T(8,128)(2,1)S(1)}, u32[]{:S(2)}, u32[]{:S(2)}) collective-permute-start(bf16[96,10,3]{2,1,0:T(8,128)(2,1)S(1)} %get-tuple-element.86), channel_id=1, source_target_pairs={{1,0},{2,1},{3,2},{5,4},{6,5},{7,6},{9,8},{10,9},{11,10},{13,12},{... | collective-permute-start | bytes 17288 | tf_op jit(solution)/shard_map/ppermute | solution.py:16
  220.4 263.3 %collective-permute-start.7 = (bf16[96,10,3]{2,1,0:T(8,128)(2,1)S(1)}, bf16[96,10,3]{2,1,0:T(8,128)(2,1)S(1)}, u32[]{:S(2)}, u32[]{:S(2)}) collective-permute-start(bf16[96,10,3]{2,1,0:T(8,128)(2,1)S(1)} %get-tuple-element.87), channel_id=1, source_target_pairs={{0,1},{1,2},{2,3},{4,5},{5,6},{6,7},{8,9},{9,10},{10,11},{12,13},{... | collective-permute-start | bytes 17288 | tf_op jit(solution)/shard_map/ppermute | solution.py:15
  (78 other events, 619.1 us)
Sparse Core Ops, SparseCore 0:
  214.8 266.9 all-reduce.3
where the time goes:
time: 506 us; the launch traced here: 505 us
  waiting for transfers between devices  268 us (53%)
  blocking collectives  109 us (22%)
  other arithmetic  66.2 us (13%)
  starting transfers between devices  22.6 us (4%)
  local copies, waits for them, and re-layouts  15.7 us (3%)
  between operations  15.6 us (3%)
  matrix products  7.76 us (2%)
    psum x1, waiting for transfers between devices, shards(): lax.psum((g_reduce, g_expand, g_ebias, g_kernel, g_dbias, norm_gain_gradi...  257 us
    psum x1, blocking collectives, shards(): lax.psum((g_reduce, g_expand, g_ebias, g_kernel, g_dbias, norm_gain_gradi...  109 us
    reduce_sum x4, other arithmetic, kernel_terms(): entries.append(jnp.sum(piece * convolution_gradient, axis=(1, 2)))  26.3 us
    ppermute x4, starting transfers between devices, padded_2(): before = lax.ppermute(last, axis, up)  13.4 us
    convert_element_type x1, other arithmetic, shards(): image_grad = (cotangent.astype(jnp.float32) + back).astype(jnp.bfloat16)  11.7 us
    reduce_sum x1, other arithmetic, shards(): average = jnp.mean(flat, axis=0, keepdims=True)  11.5 us
  transfers between devices with their start and end apart: 9, of which 4 were waited for; matrix products, arithmetic and copies ran while one was open for 2% of the time, Pallas kernels for 0%

commit v1 on v0

--- a/solution.py
+++ b/solution.py
@@ -3,6 +3,8 @@
 import jax.numpy as jnp
 from jax import lax
 from jax.sharding import PartitionSpec as P
+
+pages_mark = lambda vector: lax.psum(lax.psum(vector, axis_name="space"), "filt")
 
 
 def padded_2(x, sides, width):
@@ -157,7 +159,7 @@
         g_lbias,
         g_scale,
         g_rbias,
-    ) = lax.psum(
+    ) = pages_mark(
         (
             g_reduce,
             g_expand,
@@ -168,8 +170,7 @@
             g_lbias,
             g_scale,
             g_rbias,
-        ),
-        ("space", "filt"),
+        )
     )
     start = lax.axis_index("filt") * panel_rows
     g_reduce = lax.dynamic_slice_in_dim(g_reduce, start, panel_rows, 0)

time: 506 us -> 2450 us (4.84)
  waiting for transfers between devices: 268 us -> 1490 us
  blocking collectives: 109 us -> 812 us
    psum x1 -> x2, waiting for transfers between devices: 257 us -> 1480 us  [the longest x1 1440 us: lax.psum(vector, axis_name='space')]
    psum x1 -> x2, blocking collectives: 109 us -> 812 us  [the longest x1 799 us: lax.psum(vector, axis_name='space')]
  transfers between devices with their start and end apart: 9 -> 10, of which waited for: 4 -> 7; matrix products, arithmetic and copies ran while one was open for 2% -> 1% of each run, Pallas kernels for 0% -> 0%
where the time goes in v1:
time: 2450 us
  waiting for transfers between devices  1490 us (61%)
  blocking collectives  812 us (33%)
  other arithmetic  67.3 us (3%)
  starting transfers between devices  35.8 us (1%)
    psum x1, waiting for transfers between devices, lax.psum(vector, axis_name='space')  1440 us
    psum x1, blocking collectives, lax.psum(vector, axis_name='space')  799 us
  transfers between devices with their start and end apart: 10, of which 7 were waited for; matrix products, arithmetic and copies ran while one was open for 1% of the time, Pallas kernels for 0%

profile of v1, /device:TPU:1, one launch (start us, length us, event | category | flops | bytes accessed | tf_op | source)
XLA Modules:
  0.0 2449.1 jit_solution(17537007055685454712)
XLA Ops:
  8.5 5.5 collective-permute-start
  14.0 4.7 collective-permute-start.1
  19.7 1.6 slice_bitcast_fusion.47
  21.5 1.5 slice_bitcast_fusion.46
  23.0 1.6 pad_maximum_fusion.2
  27.4 2.0 multiply_reduce_fusion.1
  30.5 6.1 collective-permute-done.2
  37.4 1.5 collective-permute-done.3
  38.9 3.4 maximum_maximum_fusion
  42.7 11.5 fusion.134
  62.2 7.8 fusion.115
  70.0 9.8 fusion.119
  79.8 2.8 fusion.73
  84.7 5.9 fusion.118
  97.4 798.7 %all-reduce = (f32[96,7,7]{0,2,1:T(8,128)S(1)}, f32[96]{0:T(128)S(1)}, f32[96]{0:T(128)S(1)}, f32[96]{0:T(128)S(1)}, f32[384]{0:T(512)S(1)}, /*index=5*/f32[96]{0:T(128)S(1)}, f32[96]{0:T(128)S(1)}) all-reduce(f32[96,7,7]{0,2,1:T(8,128)S(1)} %constant_dynamic-update-slice_fusion, ...), channel_id=1, replica_groups=mesh['space'=128,'filt'=4] {'space'}, use_global_device_ids=true, to_apply=%region_53.0 | all-reduce | flops 5568 | bytes 44544 | tf_op jit(solution)/shard_map/psum | solution.py:7
  896.1 13.5 all-reduce.2
  912.3 6.8 collective-permute-start.4
  919.1 10.1 collective-permute-start.5
  932.2 4.7 collective-permute-start.7
  938.6 4.5 collective-permute-done.6
  944.0 3.4 pad_maximum_fusion.1
  947.4 1439.8 %all-reduce.7.cloned.1.call-done = (f32[384,96]{1,0:T(8,128)}, f32[384,96]{1,0:T(8,128)}) async-done(((f32[384,96]{1,0:T(8,128)}, f32[384,96]{1,0:T(8,128)}), (f32[384,96]{1,0:T(8,128)}, f32[384,96]{1,0:T(8,128)})) %all-reduce.7.cloned.1.call-update) | async-done | bytes 294928 | tf_op jit(solution)/shard_map/psum | solution.py:7
  2387.5 11.7 add_convert_fusion
  2399.2 41.5 %all-reduce.9.cloned.1.call-done = (f32[384,96]{1,0:T(8,128)}, f32[384,96]{1,0:T(8,128)}) async-done(((f32[384,96]{1,0:T(8,128)}, f32[384,96]{1,0:T(8,128)}), (f32[384,96]{1,0:T(8,128)}, f32[384,96]{1,0:T(8,128)})) %all-reduce.9.cloned.1.call-update) | async-done | bytes 294928 | tf_op jit(solution)/shard_map/psum | solution.py:7
  (248 shorter events, 33.1 us)
Async XLA Ops:
  7.2 2379.9 %all-reduce.7.cloned.1.call-start = ((), (), s32[]{:S(2)}) async-start(), calls=%async_computation | async-start | bytes 786432 | tf_op jit(solution)/shard_map/psum | solution.py:7
  8.5 14.5 collective-permute-start
  14.0 9.0 collective-permute-start.1
  24.8 11.9 collective-permute-start.2
  26.1 12.8 collective-permute-start.3
  912.3 17.4 collective-permute-start.4
  919.1 11.1 collective-permute-start.5
  929.1 1511.6 %all-reduce.9.cloned.1.call-start = ((), (), s32[]{:S(2)}) async-start(), calls=%async_computation.1 | async-start | bytes 786432 | tf_op jit(solution)/shard_map/psum | solution.py:7
  930.9 12.2 collective-permute-start.6
  932.2 11.8 collective-permute-start.7
  938.3 1448.9 %copy-start.24 = (f32[96]{0:T(128)S(1)}, f32[96]{0:T(128)}, u32[]{:S(2)}) copy-start(f32[96]{0:T(128)} %copy-done.23) | copy-start | bytes 1156
  938.3 1448.9 %copy-start.26 = (f32[96]{0:T(128)S(1)}, f32[96]{0:T(128)}, u32[]{:S(2)}) copy-start(f32[96]{0:T(128)} %copy-done.25) | copy-start | bytes 1156
  938.3 1448.9 %copy-start.28 = (f32[96]{0:T(128)S(1)}, f32[96]{0:T(128)}, u32[]{:S(2)}) copy-start(f32[96]{0:T(128)} %copy-done.27) | copy-start | bytes 1156
  938.3 1448.9 %copy-start.30 = (f32[96]{0:T(128)S(1)}, f32[96]{0:T(128)}, u32[]{:S(2)}) copy-start(f32[96]{0:T(128)} %copy-done.29) | copy-start | bytes 1156
  938.3 1448.9 %copy-start.32 = (f32[96]{0:T(128)S(1)}, f32[96]{0:T(128)}, u32[]{:S(2)}) copy-start(f32[96]{0:T(128)} %copy-done.31) | copy-start | bytes 1156
  938.4 1448.9 %copy-start.34 = (f32[96]{0:T(128)S(1)}, f32[96]{0:T(128)}, u32[]{:S(2)}) copy-start(f32[96]{0:T(128)} %copy-done.33) | copy-start | bytes 1156
  938.4 1448.9 %copy-start.36 = (f32[96]{0:T(128)S(1)}, f32[96]{0:T(128)}, u32[]{:S(2)}) copy-start(f32[96]{0:T(128)} %copy-done.35) | copy-start | bytes 1156
  938.4 1448.9 %copy-start.38 = (f32[96]{0:T(128)S(1)}, f32[96]{0:T(128)}, u32[]{:S(2)}) copy-start(f32[96]{0:T(128)} %copy-done.37) | copy-start | bytes 1156
  938.4 1448.9 %copy-start.40 = (f32[96]{0:T(128)S(1)}, f32[96]{0:T(128)}, u32[]{:S(2)}) copy-start(f32[96]{0:T(128)} %copy-done.39) | copy-start | bytes 1156
  938.4 1448.9 %copy-start.42 = (f32[96]{0:T(128)S(1)}, f32[96]{0:T(128)}, u32[]{:S(2)}) copy-start(f32[96]{0:T(128)} %copy-done.41) | copy-start | bytes 1156
  938.4 1448.9 %copy-start.44 = (f32[96]{0:T(128)S(1)}, f32[96]{0:T(128)}, u32[]{:S(2)}) copy-start(f32[96]{0:T(128)} %copy-done.43) | copy-start | bytes 1156
  938.4 1448.9 %copy-start.46 = (f32[96]{0:T(128)S(1)}, f32[96]{0:T(128)}, u32[]{:S(2)}) copy-start(f32[96]{0:T(128)} %copy-done.45) | copy-start | bytes 1156
  938.4 1448.9 %copy-start.48 = (f32[96]{0:T(128)S(1)}, f32[96]{0:T(128)}, u32[]{:S(2)}) copy-start(f32[96]{0:T(128)} %copy-done.47) | copy-start | bytes 1156
  938.4 1448.9 %copy-start.50 = (f32[96]{0:T(128)S(1)}, f32[96]{0:T(128)}, u32[]{:S(2)}) copy-start(f32[96]{0:T(128)} %copy-done.49) | copy-start | bytes 1156
  (80 other events, 34362.6 us)
Sparse Core Ops, SparseCore 0:
  929.3 1457.8 all-reduce.6
  2390.4 50.3 all-reduce.8
